TPU v7x, 256 devices: a whole 4x4x8 slice. The times are simulated.
256 devices in a mesh: row: 8 (over y, core), col: 32 (over x, z).
Axes of the slice: x: 4, y: 4, z: 8, core: 2. Of those that a mesh axis runs over, the one named last changes fastest.
Arguments:
- sources: float32 [65536, 256], P(('row', 'col')), may hold values from -6 to 6
- targets: float32 [65536, 256], P(('col', 'row')), may hold values from -6 to 6
- g_pot: float32 [65536], P(('col', 'row')), may hold values from -1 to 12
- log_a: float32 [65536], P(('row', 'col')), may hold values from -14 to -8
- log_b: float32 [65536], P(('col', 'row')), may hold values from -14 to -8
- src_block: int32 [16384], P(('row', 'col')), may hold values from 0 to 31, as said below
- tgt_block: int32 [16384], P(('row', 'col')), may hold values from 0 to 7, as said below
- pair_count: int32 [256], P(('row', 'col')), may hold values from 16 to 64, as said below
Outputs:
- f_new: float32 [65536], P(('row', 'col'))
- g_new: float32 [65536], P(('col', 'row'))
Inputs may be any that keep to these rules, and one draw needn't show every extreme that they name: `src_block`: within each row index, slot 0 of the 32 devices names together every source block of that row index once; slot k and slot k + 32 of a device name the same source block. `tgt_block`: within each col index, slot 0 of the 8 devices names together every target block of that col index once. `pair_count`: some device has all 64 slots live.
All inputs are finite; a program needn't handle non-finite values.
Results may differ from a plain program's by a relative error of at most 0.0003.
Values sent between devices are 32-bit elements; how exact they have to be, the bound alone decides.
A program may use at most 128 MiB of HBM per device.

v0:
```python
import jax
import jax.numpy as jnp
from jax import lax
from jax.sharding import PartitionSpec as P

BLK = 256
entropy = 0.05
lowest = -1e30


def squares_of(rows):
    return jnp.sum(rows * rows, axis=-1)


def cost_blocks(src_rows, tgt_rows, src_sq, tgt_sq):
    inner = jnp.einsum("kid,kjd->kij", src_rows, tgt_rows, precision=lax.Precision.HIGHEST)
    return (src_sq[:, :, None] + tgt_sq[:, None, :] - 2.0 * inner) / src_rows.shape[2]


def fold_blocks(slot_top, slot_total, slot_ids, alive, count):
    onehot = (slot_ids[:, None] == jnp.arange(count, dtype=jnp.int32)[None, :]) & alive[:, None]
    masked = jnp.where(onehot.T[:, :, None], slot_top[None, :, :], lowest)
    top = jnp.max(masked, axis=1)
    back = jnp.take(top, slot_ids, axis=0)
    weighted = jnp.where(alive[:, None], slot_total * jnp.exp(slot_top - back), 0.0)
    total = jnp.dot(onehot.T.astype(jnp.float32), weighted, precision=lax.Precision.HIGHEST)
    return (top.reshape(-1), total.reshape(-1))


def local(sources, targets, g_pot, log_a, log_b, src_block, tgt_block, pair_count):
    used_pairs = pair_count[0]
    slots = src_block.shape[0]
    alive = jnp.arange(slots, dtype=jnp.int32) < used_pairs
    tgt_all, pot_all = (
        lax.all_gather(targets, "row", axis=0, tiled=True),
        lax.all_gather(g_pot, "row", axis=0, tiled=True),
    )
    src_all, weight_all = (
        lax.all_gather(sources, "col", axis=0, tiled=True),
        lax.all_gather(log_a, "col", axis=0, tiled=True),
    )
    width = sources.shape[1]
    src_count = src_all.shape[0] // BLK
    tgt_count = tgt_all.shape[0] // BLK
    src_blocks = src_all.reshape(src_count, BLK, width)
    tgt_blocks = tgt_all.reshape(tgt_count, BLK, width)
    src_sq_all = squares_of(src_blocks)
    tgt_sq_all = squares_of(tgt_blocks)
    src_rows = jnp.take(src_blocks, src_block, axis=0)
    tgt_rows = jnp.take(tgt_blocks, tgt_block, axis=0)
    src_sq = jnp.take(src_sq_all, src_block, axis=0)
    tgt_sq = jnp.take(tgt_sq_all, tgt_block, axis=0)
    pot_rows = jnp.take(pot_all.reshape(tgt_count, BLK), tgt_block, axis=0)
    costs = cost_blocks(src_rows, tgt_rows, src_sq, tgt_sq)
    scores = (pot_rows[:, None, :] - costs) / entropy
    slot_top = jnp.max(scores, axis=2)
    slot_total = jnp.sum(jnp.exp(scores - slot_top[:, :, None]), axis=2)
    src_top, src_total = fold_blocks(slot_top, slot_total, src_block, alive, src_count)
    whole_top = lax.pmax(src_top, "col")
    src_total = lax.psum(src_total * jnp.exp(src_top - whole_top), "col")
    src_top = whole_top
    f_all = entropy * weight_all - entropy * (src_top + jnp.log(src_total))
    second_costs = cost_blocks(src_rows, tgt_rows, src_sq, tgt_sq)
    f_rows = jnp.take(f_all.reshape(src_count, BLK), src_block, axis=0)
    back_scores = (f_rows[:, :, None] - second_costs) / entropy
    col_top = jnp.max(back_scores, axis=1)
    col_total = jnp.sum(jnp.exp(back_scores - col_top[:, None, :]), axis=1)
    tgt_top, tgt_total = fold_blocks(col_top, col_total, tgt_block, alive, tgt_count)
    whole_tgt = lax.pmax(tgt_top, "row")
    tgt_total = lax.psum(tgt_total * jnp.exp(tgt_top - whole_tgt), "row")
    tgt_top = whole_tgt
    own_src = sources.shape[0]
    own_tgt = targets.shape[0]
    f_own = lax.dynamic_slice_in_dim(f_all, lax.axis_index("col") * own_src, own_src, 0)
    tgt_offset = lax.axis_index("row") * own_tgt
    top_own = lax.dynamic_slice_in_dim(tgt_top, tgt_offset, own_tgt, 0)
    total_own = lax.dynamic_slice_in_dim(tgt_total, tgt_offset, own_tgt, 0)
    g_own = entropy * log_b - entropy * (top_own + jnp.log(total_own))
    return (f_own, g_own)


def solution(mesh):
    placed = (
        P(("row", "col"), None),
        P(("col", "row"), None),
        P(("col", "row")),
        P(("row", "col")),
        P(("col", "row")),
        P(("row", "col")),
        P(("row", "col")),
        P(("row", "col")),
    )
    return jax.shard_map(
        local,
        mesh=mesh,
        in_specs=placed,
        out_specs=(P(("row", "col")), P(("col", "row"))),
        check_vma=False,
    )
```

profile of v0, /device:TPU:1, one launch (start us, length us, event | category | flops | bytes accessed | tf_op | source)
XLA Modules:
  0.0 527.1 jit_solution(1191801241612126786)
XLA Ops:
  7.2 0.0 all-gather.7.cloned.1.call-start
  7.2 0.7 all-gather.7.cloned.1.call-update
  7.9 0.0 all-gather.5.cloned.1.call-start
  7.9 0.7 all-gather.5.cloned.1.call-update
  8.7 12.4 %all-gather.1 = f32[8,1,256]{2,1,0:T(1,128)S(1)} all-gather(f32[1,1,256]{2,1,0:T(1,128)} %bitcast.32), channel_id=1, replica_groups=mesh['row'=8,'col'=32] {'row'}, dimensions={0}, use_global_device_ids=true | all-gather | bytes 9216 | tf_op jit(solution)/shard_map/all_gather | solution.py:36
  21.7 0.7 compare_select_fusion.1
  22.4 0.7 gather_fusion.2
  23.0 37.7 %all-gather = f32[32,1,256]{2,1,0:T(1,128)S(1)} all-gather(f32[1,1,256]{2,1,0:T(1,128)} %bitcast.33), channel_id=1, replica_groups=mesh['row'=8,'col'=32] {'col'}, dimensions={0}, use_global_device_ids=true | all-gather | bytes 33792 | tf_op jit(solution)/shard_map/all_gather | solution.py:40
  60.8 0.7 compare_select_fusion
  61.4 0.7 compare_and_fusion.1
  62.1 0.7 compare_and_fusion
  62.8 0.7 fusion.37
  63.4 0.7 fusion.36
  64.1 0.0 all-gather.7.cloned.1.call-done
  64.2 1.9 multiply_reduce_fusion.1
  66.1 0.7 gather_fusion.4
  66.8 10.5 %gather_fusion.1 = f32[64,256,256]{2,1,0:T(8,128)} fusion(f32[8,256,256]{2,1,0:T(8,128)} %bitcast.20, s32[1024]{0:T(1024)S(1)} %pad_clamp_fusion.1), kind=kCustom, calls=%fused_computation.7 | custom fusion | bytes 33554688 | tf_op jit(solution)/shard_map/jit(_take)/gather | solution.py:50
  77.3 0.1 broadcast_select_fusion.3
  77.3 64.3 %all-gather.5.cloned.1.call-done = f32[8192,256]{1,0:T(8,128)} async-done(((f32[256,256]{1,0:T(8,128)}), f32[8192,256]{1,0:T(8,128)}) %all-gather.5.cloned.1.call-update) | async-done | bytes 8388624 | tf_op jit(solution)/shard_map/all_gather | solution.py:39
  141.6 4.5 multiply_reduce_fusion
  146.2 0.7 gather_fusion.3
  146.8 11.6 %gather_fusion = f32[64,256,256]{2,1,0:T(8,128)} fusion(f32[32,256,256]{2,1,0:T(8,128)} %bitcast.21, s32[1024]{0:T(1024)S(1)} %pad_clamp_fusion), kind=kCustom, calls=%fused_computation.6 | custom fusion | bytes 33554688 | tf_op jit(solution)/shard_map/jit(_take)/gather | solution.py:49
  158.5 0.1 broadcast_select_fusion.2
  158.5 29.9 %fusion.3 = (f32[64,256]{1,0:T(8,128)S(1)}, f32[64,256,256]{2,1,0:T(8,128)}) fusion(f32[64,256]{1,0:T(8,128)S(1)} %get-tuple-element.4, f32[64,256,256]{2,1,0:T(8,128)} %gather_fusion.1, pred[64]{0:T(512)(128)(4,1)S(1)} %compare_and_fusion.1, f32[64,256,256]{2,1,0:T(8,128)} %gather_fusion, pred[64]{0:T(512)(128)(4,1)S(1)} %compare_and_fusion, ...), kind=kOutput, calls=%fused_computation.16 | convolution fusion | flops 12922634240 | bytes 50593920 | tf_op jit(solution)/shard_map/kid,kjd->kij/dot_general | solution.py:16
  188.4 0.0 copy-start.1
  188.4 8.5 %exponential_reduce_fusion.1 = f32[64,256]{1,0:T(8,128)S(1)} fusion(f32[64,256,256]{2,1,0:T(8,128)} %get-tuple-element.7, f32[64,256]{1,0:T(8,128)S(1)} %get-tuple-element.6, f32[64,256]{1,0:T(8,128)S(1)} %get-tuple-element.4), kind=kLoop, calls=%fused_computation.10 | loop fusion | flops 16760832 | bytes 16973824 | tf_op jit(solution)/shard_map/reduce_sum | solution.py:57
  197.0 0.5 select_reduce_fusion
  197.5 0.7 gather_fusion.5
  198.2 0.0 copy-done.1
  198.2 0.3 convolution_bitcast_fusion
  198.5 111.5 %pmax.14 = f32[8192]{0:T(1024)S(1)} all-reduce(f32[8192]{0:T(1024)S(1)} %bitcast.25), channel_id=1, replica_groups=mesh['row'=8,'col'=32] {'col'}, use_global_device_ids=true, to_apply=%region_4.7 | all-reduce | flops 8192 | bytes 65536 | tf_op jit(solution)/shard_map/pmax | solution.py:59
  310.0 110.7 %psum.14 = f32[8192]{0:T(1024)S(1)} all-reduce(f32[8192]{0:T(1024)S(1)} %exponential_multiply_fusion), channel_id=1, replica_groups=mesh['row'=8,'col'=32] {'col'}, use_global_device_ids=true, to_apply=%region_6.9 | all-reduce | flops 8192 | bytes 65536 | tf_op jit(solution)/shard_map/psum | solution.py:60
  420.8 0.7 gather_fusion.6
  421.4 0.1 broadcast_select_fusion
  421.5 0.0 copy-start.2
  421.5 0.0 copy-start
  421.5 7.2 %fusion.4 = f32[64,256]{1,0:T(8,128)S(1)} fusion(f32[64,256,256]{2,1,0:T(8,128)} %get-tuple-element.7, f32[64,256]{1,0:T(8,128)S(1)} %broadcast_select_fusion), kind=kLoop, calls=%fused_computation.17 | loop fusion | flops 12566528 | bytes 16908288 | tf_op jit(solution)/shard_map/reduce_max | solution.py:66
  428.8 8.0 %exponential_reduce_fusion = f32[64,256]{1,0:T(8,128)S(1)} fusion(f32[64,256,256]{2,1,0:T(8,128)} %get-tuple-element.7, f32[64,256]{1,0:T(8,128)S(1)} %fusion.4, f32[64,256]{1,0:T(8,128)S(1)} %broadcast_select_fusion), kind=kLoop, calls=%fused_computation.8 | loop fusion | flops 16760832 | bytes 16973824 | tf_op jit(solution)/shard_map/reduce_sum | solution.py:67
  436.8 0.1 select_reduce_fusion.1
  437.0 0.7 gather_fusion.7
  437.6 0.0 copy-done.2
  437.6 0.3 convolution_bitcast_fusion.1
  437.9 68.4 %pmax.15 = f32[2048]{0:T(1024)S(1)} all-reduce(f32[2048]{0:T(1024)S(1)} %bitcast.29), channel_id=1, replica_groups=mesh['row'=8,'col'=32] {'row'}, use_global_device_ids=true, to_apply=%region_9.12 | all-reduce | flops 2048 | bytes 16384 | tf_op jit(solution)/shard_map/pmax | solution.py:69
  506.3 12.7 %psum.15 = f32[2048]{0:T(1024)S(1)} all-reduce(f32[2048]{0:T(1024)S(1)} %exponential_multiply_fusion.1), channel_id=1, replica_groups=mesh['row'=8,'col'=32] {'row'}, use_global_device_ids=true, to_apply=%region_11.14 | all-reduce | flops 2048 | bytes 16384 | tf_op jit(solution)/shard_map/psum | solution.py:70
  519.0 0.6 dynamic_slice.9
  519.7 0.0 copy-done
  519.7 0.6 multiply_subtract_fusion.1
  (15 shorter events, 0.2 us)
Async XLA Ops:
  7.2 57.0 %all-gather.7.cloned.1.call-start = ((), (), s32[]{:S(2)}) async-start(), calls=%async_computation.1 | async-start | bytes 2359296 | tf_op jit(solution)/shard_map/all_gather | solution.py:35
  7.9 133.7 %all-gather.5.cloned.1.call-start = ((), (), s32[]{:S(2)}) async-start(), calls=%async_computation | async-start | bytes 8650752 | tf_op jit(solution)/shard_map/all_gather | solution.py:39
  188.4 9.7 %copy-start.1 = (s32[64]{0:T(128)S(1)}, s32[64]{0:T(128)}, u32[]{:S(2)}) copy-start(s32[64]{0:T(128)} %param.17) | copy-start | bytes 772
  421.5 16.1 %copy-start.2 = (s32[64]{0:T(128)S(1)}, s32[64]{0:T(128)}, u32[]{:S(2)}) copy-start(s32[64]{0:T(128)} %param.18) | copy-start | bytes 772
  421.5 98.1 %copy-start = (f32[256]{0:T(256)S(1)}, f32[256]{0:T(256)}, u32[]{:S(2)}) copy-start(f32[256]{0:T(256)} %param.16) | copy-start | bytes 3076
Sparse Core Ops, SparseCore 0:
  9.8 32.0 all-gather.6
  44.5 97.0 all-gather.4
where the time goes:
time: 528 us; the launch traced here: 527 us
  blocking collectives  353 us (67%)
  waiting for transfers between devices  65.7 us (12%)
  other arithmetic  35.9 us (7%)
  matrix products  30.4 us (6%)
  local copies, waits for them, and re-layouts  26.8 us (5%)
  between operations  14.9 us (3%)
    pmax x1, blocking collectives, local(): whole_top = lax.pmax(src_top, 'col')  112 us
    psum x1, blocking collectives, local(): src_total = lax.psum(src_total * jnp.exp(src_top - whole_top), 'col')  111 us
    pmax x1, blocking collectives, local(): whole_tgt = lax.pmax(tgt_top, 'row')  68.4 us
    all_gather x1, waiting for transfers between devices, local(): lax.all_gather(sources, 'col', axis=0, tiled=True)  64.3 us
    all_gather x1, blocking collectives, local(): lax.all_gather(log_a, 'col', axis=0, tiled=True)  37.7 us
    dot_general x1, matrix products, cost_blocks(): jnp.einsum('kid,kjd->kij', src_rows, tgt_rows, precision=lax.Precision.HI...  29.9 us
    psum x1, blocking collectives, local(): tgt_total = lax.psum(tgt_total * jnp.exp(tgt_top - whole_tgt), 'row')  12.7 us
    all_gather x1, blocking collectives, local(): lax.all_gather(g_pot, 'row', axis=0, tiled=True)  12.4 us
  transfers between devices with their start and end apart: 2, of which 1 were waited for; matrix products, arithmetic and copies ran while one was open for 3% of the time, Pallas kernels for 0%

commit v1 on v0

--- a/solution.py
+++ b/solution.py
@@ -6,6 +6,12 @@
 BLK = 256
 entropy = 0.05
 lowest = -1e30
+
+
+def produce_notes_on(x_part, comm_axis, axis_k):
+    then = jnp.stack([x_part for _ in range(lax.psum(1, comm_axis))])
+    new = lax.all_to_all(then, axis_name=comm_axis, split_axis=0, concat_axis=0)
+    return jnp.concatenate(new, axis=axis_k)
 
 
 def squares_of(rows):
@@ -37,7 +43,7 @@
     )
     src_all, weight_all = (
         lax.all_gather(sources, "col", axis=0, tiled=True),
-        lax.all_gather(log_a, "col", axis=0, tiled=True),
+        produce_notes_on(log_a, "col", 0),
     )
     width = sources.shape[1]
     src_count = src_all.shape[0] // BLK

time: 528 us -> 528 us (level)
  blocking collectives: 353 us -> 315 us
  waiting for transfers between devices: 65.7 us -> 90.7 us
  starting transfers between devices: 0.08 us -> 11.9 us
    all_gather x1 -> x0, blocking collectives: 37.7 us -> none  [local(): lax.all_gather(log_a, 'col', axis=0, tiled=True)]
    all_gather x1, waiting for transfers between devices: 64.3 us -> 86.5 us  [local(): lax.all_gather(sources, 'col', axis=0, tiled=True)]
    all_to_all x0 -> x1, starting transfers between devices: none -> 11.9 us  [produce_notes_on(): new = lax.all_to_all(then, axis_name=comm_axis, split_axis=0, concat_axis=0)]
  transfers between devices with their start and end apart: 2 -> 3, of which waited for: 1 -> 2; matrix products, arithmetic and copies ran while one was open for 3% -> 4% of each run, Pallas kernels for 0% -> 0%
where the time goes in v1:
time: 528 us; the launch traced here: 527 us
  blocking collectives  315 us (60%)
  waiting for transfers between devices  90.7 us (17%)
  other arithmetic  35.9 us (7%)
  matrix products  30.4 us (6%)
  local copies, waits for them, and re-layouts  28 us (5%)
  between operations  14.9 us (3%)
  starting transfers between devices  11.9 us (2%)
    pmax x1, blocking collectives, local(): whole_top = lax.pmax(src_top, 'col')  112 us
    psum x1, blocking collectives, local(): src_total = lax.psum(src_total * jnp.exp(src_top - whole_top), 'col')  111 us
    all_gather x1, waiting for transfers between devices, local(): lax.all_gather(sources, 'col', axis=0, tiled=True)  86.5 us
    pmax x1, blocking collectives, local(): whole_tgt = lax.pmax(tgt_top, 'row')  68.4 us
    dot_general x1, matrix products, cost_blocks(): jnp.einsum('kid,kjd->kij', src_rows, tgt_rows, precision=lax.Precision.HI...  29.9 us
    psum x1, blocking collectives, local(): tgt_total = lax.psum(tgt_total * jnp.exp(tgt_top - whole_tgt), 'row')  12.7 us
    all_gather x1, blocking collectives, local(): lax.all_gather(g_pot, 'row', axis=0, tiled=True)  12 us
    all_to_all x1, starting transfers between devices, produce_notes_on(): new = lax.all_to_all(then, axis_name=comm_axis, split_axis=0, concat_axis=0)  11.9 us
  transfers between devices with their start and end apart: 3, of which 2 were waited for; matrix products, arithmetic and copies ran while one was open for 4% of the time, Pallas kernels for 0%

profile of v1, /device:TPU:1, one launch (start us, length us, event | category | flops | bytes accessed | tf_op | source)
XLA Modules:
  0.0 527.1 jit_solution(12471940825700368541)
XLA Ops:
  7.2 0.0 all-gather.6.cloned.1.call-start
  7.2 0.7 all-gather.6.cloned.1.call-update
  7.9 0.0 all-gather.4.cloned.1.call-start
  7.9 0.7 all-gather.4.cloned.1.call-update
  8.6 1.3 stack.2
  9.9 11.9 %all-to-all-start = ((f32[32,1,256]{2,1,0:T(1,128)}), f32[32,1,256]{2,1,0:T(1,128)S(1)}, u32[]{:S(2)}, u32[]{:S(2)}) async-start(f32[32,1,256]{2,1,0:T(1,128)} %stack.2), calls=%async_computation | async-start | bytes 65536 | tf_op jit(solution)/shard_map/all_to_all | solution.py:13
  21.8 12.0 %all-gather = f32[8,1,256]{2,1,0:T(1,128)S(1)} all-gather(f32[1,1,256]{2,1,0:T(1,128)} %bitcast.31), channel_id=1, replica_groups=mesh['row'=8,'col'=32] {'row'}, dimensions={0}, use_global_device_ids=true | all-gather | bytes 9216 | tf_op jit(solution)/shard_map/all_gather | solution.py:42
  34.5 0.7 compare_select_fusion.1
  35.1 0.7 gather_fusion.2
  35.8 0.7 compare_and_fusion.1
  36.5 0.7 compare_select_fusion
  37.1 0.7 compare_and_fusion
  37.8 0.7 fusion.37
  38.5 0.7 fusion.36
  39.1 0.0 all-to-all-done
  39.2 2.7 all-gather.6.cloned.1.call-done
  41.9 1.9 multiply_reduce_fusion.1
  43.9 0.7 gather_fusion.4
  44.5 10.4 %gather_fusion.1 = f32[64,256,256]{2,1,0:T(8,128)} fusion(f32[8,256,256]{2,1,0:T(8,128)} %bitcast.19, s32[1024]{0:T(1024)S(1)} %pad_clamp_fusion.1), kind=kCustom, calls=%fused_computation.7 | custom fusion | bytes 33554688 | tf_op jit(solution)/shard_map/jit(_take)/gather | solution.py:56
  54.9 0.1 broadcast_select_fusion.3
  55.0 86.5 %all-gather.4.cloned.1.call-done = f32[8192,256]{1,0:T(8,128)} async-done(((f32[256,256]{1,0:T(8,128)}), f32[8192,256]{1,0:T(8,128)}) %all-gather.4.cloned.1.call-update) | async-done | bytes 8388624 | tf_op jit(solution)/shard_map/all_gather | solution.py:45
  141.6 4.5 multiply_reduce_fusion
  146.1 0.7 gather_fusion.3
  146.8 11.6 %gather_fusion = f32[64,256,256]{2,1,0:T(8,128)} fusion(f32[32,256,256]{2,1,0:T(8,128)} %bitcast.20, s32[1024]{0:T(1024)S(1)} %pad_clamp_fusion), kind=kCustom, calls=%fused_computation.6 | custom fusion | bytes 33554688 | tf_op jit(solution)/shard_map/jit(_take)/gather | solution.py:55
  158.4 0.1 broadcast_select_fusion.2
  158.5 29.9 %fusion.3 = (f32[64,256]{1,0:T(8,128)S(1)}, f32[64,256,256]{2,1,0:T(8,128)}) fusion(f32[64,256]{1,0:T(8,128)S(1)} %get-tuple-element.4, f32[64,256,256]{2,1,0:T(8,128)} %gather_fusion.1, pred[64]{0:T(512)(128)(4,1)S(1)} %compare_and_fusion.1, f32[64,256,256]{2,1,0:T(8,128)} %gather_fusion, pred[64]{0:T(512)(128)(4,1)S(1)} %compare_and_fusion, ...), kind=kOutput, calls=%fused_computation.16 | convolution fusion | flops 12922634240 | bytes 50593920 | tf_op jit(solution)/shard_map/kid,kjd->kij/dot_general | solution.py:22
  188.4 8.5 %exponential_reduce_fusion.1 = f32[64,256]{1,0:T(8,128)S(1)} fusion(f32[64,256,256]{2,1,0:T(8,128)} %get-tuple-element.7, f32[64,256]{1,0:T(8,128)S(1)} %get-tuple-element.6, f32[64,256]{1,0:T(8,128)S(1)} %get-tuple-element.4), kind=kLoop, calls=%fused_computation.10 | loop fusion | flops 16760832 | bytes 16973824 | tf_op jit(solution)/shard_map/reduce_sum | solution.py:63
  196.9 0.5 select_reduce_fusion
  197.4 0.7 gather_fusion.5
  198.1 0.0 copy-done.1
  198.1 0.3 convolution_bitcast_fusion
  198.4 111.5 %pmax.14 = f32[8192]{0:T(1024)S(1)} all-reduce(f32[8192]{0:T(1024)S(1)} %bitcast.24), channel_id=1, replica_groups=mesh['row'=8,'col'=32] {'col'}, use_global_device_ids=true, to_apply=%region_4.7 | all-reduce | flops 8192 | bytes 65536 | tf_op jit(solution)/shard_map/pmax | solution.py:65
  310.0 110.7 %psum.14 = f32[8192]{0:T(1024)S(1)} all-reduce(f32[8192]{0:T(1024)S(1)} %exponential_multiply_fusion), channel_id=1, replica_groups=mesh['row'=8,'col'=32] {'col'}, use_global_device_ids=true, to_apply=%region_6.9 | all-reduce | flops 8192 | bytes 65536 | tf_op jit(solution)/shard_map/psum | solution.py:66
  420.7 0.7 gather_fusion.6
  421.4 0.1 broadcast_select_fusion
  421.5 0.0 copy-start.2
  421.5 0.0 copy-start
  421.5 7.2 %fusion.4 = f32[64,256]{1,0:T(8,128)S(1)} fusion(f32[64,256,256]{2,1,0:T(8,128)} %get-tuple-element.7, f32[64,256]{1,0:T(8,128)S(1)} %broadcast_select_fusion), kind=kLoop, calls=%fused_computation.17 | loop fusion | flops 12566528 | bytes 16908288 | tf_op jit(solution)/shard_map/reduce_max | solution.py:72
  428.7 8.0 %exponential_reduce_fusion = f32[64,256]{1,0:T(8,128)S(1)} fusion(f32[64,256,256]{2,1,0:T(8,128)} %get-tuple-element.7, f32[64,256]{1,0:T(8,128)S(1)} %fusion.4, f32[64,256]{1,0:T(8,128)S(1)} %broadcast_select_fusion), kind=kLoop, calls=%fused_computation.8 | loop fusion | flops 16760832 | bytes 16973824 | tf_op jit(solution)/shard_map/reduce_sum | solution.py:73
  436.8 0.1 select_reduce_fusion.1
  436.9 0.7 gather_fusion.7
  437.6 0.0 copy-done.2
  437.6 0.3 convolution_bitcast_fusion.1
  437.9 68.4 %pmax.15 = f32[2048]{0:T(1024)S(1)} all-reduce(f32[2048]{0:T(1024)S(1)} %bitcast.28), channel_id=1, replica_groups=mesh['row'=8,'col'=32] {'row'}, use_global_device_ids=true, to_apply=%region_9.12 | all-reduce | flops 2048 | bytes 16384 | tf_op jit(solution)/shard_map/pmax | solution.py:75
  506.3 12.7 %psum.15 = f32[2048]{0:T(1024)S(1)} all-reduce(f32[2048]{0:T(1024)S(1)} %exponential_multiply_fusion.1), channel_id=1, replica_groups=mesh['row'=8,'col'=32] {'row'}, use_global_device_ids=true, to_apply=%region_11.14 | all-reduce | flops 2048 | bytes 16384 | tf_op jit(solution)/shard_map/psum | solution.py:76
  519.0 0.6 dynamic_slice.9
  519.6 0.0 copy-done
  519.6 0.6 multiply_subtract_fusion.1
  (16 shorter events, 0.2 us)
Async XLA Ops:
  7.2 34.8 %all-gather.6.cloned.1.call-start = ((), (), s32[]{:S(2)}) async-start(), calls=%async_computation.2 | async-start | bytes 2359296 | tf_op jit(solution)/shard_map/all_gather | solution.py:41
  7.9 133.7 %all-gather.4.cloned.1.call-start = ((), (), s32[]{:S(2)}) async-start(), calls=%async_computation.1 | async-start | bytes 8650752 | tf_op jit(solution)/shard_map/all_gather | solution.py:45
  9.9 29.2 %all-to-all-start = ((f32[32,1,256]{2,1,0:T(1,128)}), f32[32,1,256]{2,1,0:T(1,128)S(1)}, u32[]{:S(2)}, u32[]{:S(2)}) async-start(f32[32,1,256]{2,1,0:T(1,128)} %stack.2), calls=%async_computation | async-start | bytes 65536 | tf_op jit(solution)/shard_map/all_to_all | solution.py:13
  188.4 9.7 %copy-start.1 = (s32[64]{0:T(128)S(1)}, s32[64]{0:T(128)}, u32[]{:S(2)}) copy-start(s32[64]{0:T(128)} %param.17) | copy-start | bytes 772
  421.5 16.1 %copy-start.2 = (s32[64]{0:T(128)S(1)}, s32[64]{0:T(128)}, u32[]{:S(2)}) copy-start(s32[64]{0:T(128)} %param.18) | copy-start | bytes 772
  421.5 98.1 %copy-start = (f32[256]{0:T(256)S(1)}, f32[256]{0:T(256)}, u32[]{:S(2)}) copy-start(f32[256]{0:T(256)} %param.16) | copy-start | bytes 3076
Sparse Core Ops, SparseCore 0:
  9.8 32.0 all-gather.5
  44.5 96.9 all-gather.3
